TPU v7x, 32 devices: a whole 2x2x4 slice. The times are simulated.
32 devices in a mesh: dp: 16 (over z, y, x), mp: 2 (over core).
Axes of the slice: x: 2, y: 2, z: 4, core: 2. Of those that a mesh axis runs over, the one named last changes fastest.
Arguments:
- tokens: bfloat16 [32768, 768], P('dp'), may hold values from -6 to 6
- segments: int32 [32768], P('dp'), may hold values from 0 to 32, as said below
- sentence_dest: int32 [2048, 2], P('dp'), may hold values from 0 to 15, as said below
- pair_source: int32 [2048, 2], P('dp'), may hold values from 0 to 15, as said below
- labels: int32 [1024], P('dp'), may hold values from 0 to 5
- params: float32 [2, 3541248], P('mp', 'dp'), as said below
- first: float32 [2, 3541248], P('mp', 'dp')
- second: float32 [2, 3541248], P('mp', 'dp'), as said below
- shared: float32 [6, 768], replicated, as said below
- shared_first: float32 [6, 768], replicated
- shared_second: float32 [6, 768], replicated, as said below
Outputs:
- encoded: bfloat16 [32768, 768], P('dp')
- input_grad: float32 [32768, 768], P('dp')
- grad_norm: float32 [1], replicated
- params_new: float32 [2, 3541248], P('mp', 'dp')
- first_new: float32 [2, 3541248], P('mp', 'dp')
- second_new: float32 [2, 3541248], P('mp', 'dp')
- params_low: bfloat16 [2, 3541248], P('mp', 'dp')
- shared_new: float32 [6, 768], replicated
- shared_first_new: float32 [6, 768], replicated
- shared_second_new: float32 [6, 768], replicated
- params_grad: float32 [2, 3541248], P('mp', 'dp')
- shared_grad: float32 [6, 768], replicated
Inputs may be any that keep to these rules, and one draw needn't show every extreme that they name: `segments`: within each row of 512 positions ids never fall; each id 0 to 31 covers 1 to 16 positions and slot 0 exactly 16; id 32 marks the padding at a row's end. `sentence_dest`: column 0 is the scoring device, column 1 the place 0 to 7 among the sentences that this device sends there; each device sends exactly 8 or none of its sentences to each device, and each (device, place) occurs once per sender. `pair_source`: column 0 is the sending device, column 1 the place; each names a sentence whose sentence_dest points to this device and place, every sentence exactly once; items 2j and 2j+1 form pair j. `params`: laid out as the steps say. `second`: Positive. `shared`: Rows: first gain, first bias, second gain, second bias, attention output bias, feed-forward output bias. `shared_second`: Positive.
All inputs are finite; a program needn't handle non-finite values.
Results may differ from a plain program's by a relative error of at most 0.018.
Values may be sent and summed in bfloat16 or wider, within the bound.
A program may use at most 256 MiB of HBM per device.

v0:
```python
from functools import partial
import math
import jax
import jax.numpy as jnp
from jax import lax
from jax.sharding import PartitionSpec as P

HEAD_DIM = 64
FF = 3072
ROW = 512
SEG = 32
RPM = 2
MB = 2
LOSS_SCALE = 1024.0
CLIP_NORM = 0.5
LEARN_RATE = 0.1
SHARED_RATE = 0.5
BETA_ONE = 0.9
BETA_TWO = 0.999
ADAM_EPS = 1e-08
DECAY = 0.01
NORM_EPS = 1e-12
STEP_COUNT = 10.0
TOP_PRECISION = lax.Precision.HIGHEST


def normalize(values_in, scale_vec, shift_vec):
    center = jnp.mean(values_in, -1, keepdims=True)
    centered = values_in - center
    spread = jnp.mean(centered * centered, -1, keepdims=True)
    return centered * lax.rsqrt(spread + NORM_EPS) * scale_vec + shift_vec


def unpack(packed, features, head_cols, ffn_cols):
    pieces = []
    offset = 0
    for height, extent in (
        (features, 3 * head_cols),
        (head_cols, features),
        (features, ffn_cols),
        (ffn_cols, features),
    ):
        pieces.append(packed[offset : offset + height * extent].reshape(height, extent))
        offset = offset + height * extent
    for extent in (head_cols, head_cols, ffn_cols):
        pieces.append(packed[offset : offset + extent])
        offset = offset + extent
    return pieces


def pair_loss(pair_items, labels):
    first_vec = pair_items[..., 0::2, :]
    second_vec = pair_items[..., 1::2, :]
    inner_prod = jnp.sum(first_vec * second_vec, -1)
    cosine = (
        inner_prod
        * lax.rsqrt(jnp.sum(first_vec * first_vec, -1) + 1e-06)
        * lax.rsqrt(jnp.sum(second_vec * second_vec, -1) + 1e-06)
    )
    error_term = cosine - labels.astype(jnp.float32) / 5.0
    return LOSS_SCALE * jnp.sum(error_term * error_term)


def adamw(weight, moment_one, moment_two, gradient, factor, step_count, rate):
    clipped = gradient * factor
    first_new = BETA_ONE * moment_one + (1.0 - BETA_ONE) * clipped
    second_new = BETA_TWO * moment_two + (1.0 - BETA_TWO) * clipped * clipped
    first_hat = first_new / (1.0 - BETA_ONE**step_count)
    second_hat = second_new / (1.0 - BETA_TWO**step_count)
    weight_new = weight - rate * (first_hat / (jnp.sqrt(second_hat) + ADAM_EPS) + DECAY * weight)
    return (weight_new, first_new, second_new)


def per_device(
    tokens,
    segments,
    sentence_dest,
    pair_source,
    labels,
    params,
    first,
    second,
    shared,
    shared_first,
    shared_second,
):
    features = tokens.shape[1]
    head_cols = features // lax.axis_size("mp")
    ffn_cols = FF // lax.axis_size("mp")
    heads_dev = head_cols // HEAD_DIM
    dp_count = lax.axis_size("dp")
    sent_slots = MB * RPM * SEG
    slot_capacity = max(2, sent_slots // dp_count)
    score_scale = HEAD_DIM ** (-0.5)
    flat_rows = RPM * ROW
    params_total = lax.axis_size("mp") * params.shape[1] * dp_count + 6 * features
    low_shard = params.astype(jnp.bfloat16)

    def weights_now():
        return unpack(
            lax.all_gather(low_shard, "dp", axis=1, tiled=True)[0], features, head_cols, ffn_cols
        )

    slot_ids = jnp.arange(SEG, dtype=jnp.int32)

    def pooling_matrix(block_segments):
        onehot = (block_segments[:, None, :] == slot_ids[None, :, None]).astype(jnp.float32)
        return onehot / jnp.sum(onehot, 2, keepdims=True)

    def masked_scores(queries, keys_low, block_segments):
        same_doc = (block_segments[:, :, None] == block_segments[:, None, :])[:, None]
        scores = (
            jnp.einsum("rqhd,rkhd->rhqk", queries, keys_low, preferred_element_type=jnp.float32)
            * score_scale
        )
        return jnp.where(same_doc, scores, -1e30)

    def forward_step(carried, inputs):
        tokens_block, block_segments = inputs
        w_qkv, w_attn, w_in, w_out, b_query, b_value, b_in = weights_now()
        tokens_flat = tokens_block.reshape(flat_rows, features)
        projected = jnp.dot(tokens_flat, w_qkv, preferred_element_type=jnp.float32)
        queries = (
            (projected[:, :head_cols] + b_query)
            .astype(jnp.bfloat16)
            .reshape(RPM, ROW, heads_dev, HEAD_DIM)
        )
        keys_low = (
            projected[:, head_cols : 2 * head_cols]
            .astype(jnp.bfloat16)
            .reshape(RPM, ROW, heads_dev, HEAD_DIM)
        )
        values_low = (
            (projected[:, 2 * head_cols :] + b_value)
            .astype(jnp.bfloat16)
            .reshape(RPM, ROW, heads_dev, HEAD_DIM)
        )
        scores = masked_scores(queries, keys_low, block_segments)
        row_max = jnp.max(scores, -1, keepdims=True)
        exponent = jnp.exp(scores - row_max)
        row_total = jnp.sum(exponent, -1, keepdims=True)
        attn_probs = (exponent / row_total).astype(jnp.bfloat16)
        log_total = row_max + jnp.log(row_total)
        mixed_heads = jnp.einsum(
            "rhqk,rkhd->rqhd", attn_probs, values_low, preferred_element_type=jnp.float32
        )
        mixed_heads = mixed_heads.reshape(flat_rows, head_cols).astype(jnp.bfloat16)
        attn_term = jnp.dot(mixed_heads, w_attn, preferred_element_type=jnp.float32)
        attn_out = lax.psum(attn_term.astype(jnp.bfloat16), "mp").astype(jnp.float32) + shared[4]
        resid_one = tokens_flat.astype(jnp.float32) + attn_out
        hidden = normalize(resid_one, shared[0], shared[1])
        up_proj = (
            jnp.dot(hidden.astype(jnp.bfloat16), w_in, preferred_element_type=jnp.float32) + b_in
        )
        activated = jax.nn.gelu(up_proj, approximate=False).astype(jnp.bfloat16)
        ffn_term = jnp.dot(activated, w_out, preferred_element_type=jnp.float32)
        ffn_out = lax.psum(ffn_term.astype(jnp.bfloat16), "mp").astype(jnp.float32) + shared[5]
        resid_two = hidden + ffn_out
        encoded_flat = normalize(resid_two, shared[2], shared[3])
        block_encodings = encoded_flat.reshape(RPM, ROW, features)
        pooled = jnp.einsum(
            "kvf,kfo->kvo", pooling_matrix(block_segments), block_encodings, precision=TOP_PRECISION
        ).astype(jnp.bfloat16)
        saved_state = (
            queries,
            keys_low,
            values_low,
            log_total,
            mixed_heads,
            resid_one,
            up_proj,
            activated,
            resid_two,
        )
        return (carried, (block_encodings.astype(jnp.bfloat16), pooled, saved_state))

    token_blocks = tokens.reshape(MB, RPM, ROW, features)
    segment_blocks = segments.reshape(MB, RPM, ROW)
    ignored, (encoded, pooled_all, saved_all) = lax.scan(
        forward_step, jnp.zeros((), jnp.float32), (token_blocks, segment_blocks)
    )
    pooled_flat = pooled_all.reshape(sent_slots, features)
    code_ids = jnp.arange(dp_count * slot_capacity, dtype=jnp.int32)
    send_code = sentence_dest[:, 0] * slot_capacity + sentence_dest[:, 1]
    send_map = (code_ids[:, None] == send_code[None, :]).astype(jnp.bfloat16)
    outgoing = jnp.dot(send_map, pooled_flat, preferred_element_type=jnp.float32).astype(
        jnp.bfloat16
    )
    outgoing = outgoing.reshape(dp_count, slot_capacity, features)
    incoming = lax.all_to_all(outgoing, "dp", split_axis=0, concat_axis=0, tiled=True).reshape(
        dp_count * slot_capacity, features
    )
    take_code = pair_source[:, 0] * slot_capacity + pair_source[:, 1]
    take_map = (take_code[:, None] == code_ids[None, :]).astype(jnp.bfloat16)
    pair_items = jnp.dot(take_map, incoming, preferred_element_type=jnp.float32)
    item_grad = jax.grad(pair_loss)(pair_items, labels).astype(jnp.bfloat16)
    returning = jnp.dot(take_map.T, item_grad, preferred_element_type=jnp.float32).astype(
        jnp.bfloat16
    )
    returning = returning.reshape(dp_count, slot_capacity, features)
    arrived = lax.all_to_all(returning, "dp", split_axis=0, concat_axis=0, tiled=True).reshape(
        dp_count * slot_capacity, features
    )
    pooled_grad = jnp.dot(send_map.T, arrived, preferred_element_type=jnp.float32).reshape(
        MB, RPM, SEG, features
    )

    def backward_step(carried, inputs):
        shared_acc, flat_acc = carried
        tokens_block, block_segments, sentence_gradient, saved_state = inputs
        (
            queries,
            keys_low,
            values_low,
            log_total,
            mixed_heads,
            resid_one,
            up_proj,
            activated,
            resid_two,
        ) = saved_state
        w_qkv, w_attn, w_in, w_out, b_query, b_value, b_in = weights_now()
        tokens_flat = tokens_block.reshape(flat_rows, features)
        encoded_grad = jnp.einsum(
            "jix,jip->jxp",
            pooling_matrix(block_segments),
            sentence_gradient,
            precision=TOP_PRECISION,
        ).reshape(flat_rows, features)
        ignored_two, norm_two_back = jax.vjp(normalize, resid_two, shared[2], shared[3])
        resid_two_grad, scale_two, shift_two = norm_two_back(encoded_grad)
        ffn_grad = resid_two_grad.astype(jnp.bfloat16)
        ignored_act, gelu_back = jax.vjp(partial(jax.nn.gelu, approximate=False), up_proj)
        act_grad = jnp.dot(ffn_grad, w_out.T, preferred_element_type=jnp.float32)
        up_grad = gelu_back(act_grad)[0].astype(jnp.bfloat16)
        hidden, norm_one_back = jax.vjp(normalize, resid_one, shared[0], shared[1])
        w_out_grad = jnp.dot(activated.T, ffn_grad, preferred_element_type=jnp.float32)
        w_in_grad = jnp.dot(
            hidden.astype(jnp.bfloat16).T, up_grad, preferred_element_type=jnp.float32
        )
        hidden_term = jnp.dot(up_grad, w_in.T, preferred_element_type=jnp.float32)
        hidden_grad = resid_two_grad + lax.psum(hidden_term.astype(jnp.bfloat16), "mp").astype(
            jnp.float32
        )
        resid_one_grad, scale_one, shift_one = norm_one_back(hidden_grad)
        attn_grad = resid_one_grad.astype(jnp.bfloat16)
        w_attn_grad = jnp.dot(mixed_heads.T, attn_grad, preferred_element_type=jnp.float32)
        mixed_grad = jnp.dot(attn_grad, w_attn.T, preferred_element_type=jnp.float32)
        mixed_grad = mixed_grad.astype(jnp.bfloat16).reshape(RPM, ROW, heads_dev, HEAD_DIM)
        attn_probs = jnp.exp(masked_scores(queries, keys_low, block_segments) - log_total)
        value_grad = jnp.einsum(
            "rhqk,rqhd->rkhd",
            attn_probs.astype(jnp.bfloat16),
            mixed_grad,
            preferred_element_type=jnp.float32,
        )
        prob_grad = jnp.einsum(
            "rqhd,rkhd->rhqk", mixed_grad, values_low, preferred_element_type=jnp.float32
        )
        row_inner = jnp.sum(prob_grad * attn_probs, -1, keepdims=True)
        score_grad = (attn_probs * (prob_grad - row_inner)).astype(jnp.bfloat16)
        query_grad = (
            jnp.einsum("rhqk,rkhd->rqhd", score_grad, keys_low, preferred_element_type=jnp.float32)
            * score_scale
        )
        key_grad = (
            jnp.einsum("rhqk,rqhd->rkhd", score_grad, queries, preferred_element_type=jnp.float32)
            * score_scale
        )
        query_key_value_gradient = jnp.concatenate(
            [
                query_grad.reshape(flat_rows, head_cols),
                key_grad.reshape(flat_rows, head_cols),
                value_grad.reshape(flat_rows, head_cols),
            ],
            1,
        ).astype(jnp.bfloat16)
        w_qkv_grad = jnp.dot(
            tokens_flat.T, query_key_value_gradient, preferred_element_type=jnp.float32
        )
        input_term = jnp.dot(query_key_value_gradient, w_qkv.T, preferred_element_type=jnp.float32)
        input_grad = resid_one_grad + lax.psum(input_term.astype(jnp.bfloat16), "mp").astype(
            jnp.float32
        )
        column_sums = jnp.sum(query_key_value_gradient.astype(jnp.float32), 0)
        grad_flat = jnp.concatenate(
            [
                w_qkv_grad.reshape(-1),
                w_attn_grad.reshape(-1),
                w_in_grad.reshape(-1),
                w_out_grad.reshape(-1),
                column_sums[:head_cols],
                column_sums[2 * head_cols :],
                jnp.sum(up_grad.astype(jnp.float32), 0),
            ]
        )[None]
        shared_step = jnp.stack(
            [
                scale_one,
                shift_one,
                scale_two,
                shift_two,
                jnp.sum(attn_grad.astype(jnp.float32), 0),
                jnp.sum(ffn_grad.astype(jnp.float32), 0),
            ]
        )
        flat_acc = flat_acc + lax.psum_scatter(grad_flat, "dp", scatter_dimension=1, tiled=True)
        return ((shared_acc + shared_step, flat_acc), input_grad)

    flat_start = jnp.zeros((1, params.shape[1]), jnp.float32)
    (shared_acc, flat_acc), input_grads = lax.scan(
        backward_step,
        (jnp.zeros_like(shared), flat_start),
        (token_blocks, segment_blocks, pooled_grad, saved_all),
    )
    flat_grad = flat_acc
    flat_grad = flat_grad / LOSS_SCALE
    local_squares = jnp.sum(flat_grad * flat_grad)
    shared_total = lax.psum(shared_acc, "dp")
    total_squares = lax.psum(local_squares, ("dp", "mp"))
    shared_grad = shared_total / LOSS_SCALE
    norm_value = jnp.sqrt(total_squares + jnp.sum(shared_grad * shared_grad))
    factor = jnp.minimum(1.0, CLIP_NORM / norm_value)
    step_count = STEP_COUNT
    params_new, first_new, second_new = adamw(
        params, first, second, flat_grad, factor, step_count, LEARN_RATE
    )
    shared_new, shared_first_new, shared_second_new = adamw(
        shared, shared_first, shared_second, shared_grad, factor, step_count, SHARED_RATE
    )
    grad_unit = math.sqrt(params_total) / CLIP_NORM
    params_grad = flat_grad * factor * grad_unit
    shared_grad_out = shared_grad * factor * grad_unit
    return (
        encoded.reshape(MB * RPM * ROW, features),
        input_grads.reshape(MB * RPM * ROW, features),
        norm_value.reshape(1),
        params_new,
        first_new,
        second_new,
        params_new.astype(jnp.bfloat16),
        shared_new,
        shared_first_new,
        shared_second_new,
        params_grad,
        shared_grad_out,
    )


def solution(mesh):
    in_specs = (
        P("dp", None),
        P("dp"),
        P("dp", None),
        P("dp", None),
        P("dp"),
        P("mp", "dp"),
        P("mp", "dp"),
        P("mp", "dp"),
        P(),
        P(),
        P(),
    )
    out_specs = (
        P("dp", None),
        P("dp", None),
        P(),
        P("mp", "dp"),
        P("mp", "dp"),
        P("mp", "dp"),
        P("mp", "dp"),
        P(),
        P(),
        P(),
        P("mp", "dp"),
        P(),
    )
    return jax.shard_map(
        per_device, mesh=mesh, in_specs=in_specs, out_specs=out_specs, check_vma=False
    )
```

profile of v0, /device:TPU:0, one launch (start us, length us, event | category | flops | bytes accessed | tf_op | source)
XLA Modules:
  0.0 3310.9 jit_solution(3628532116276965584)
XLA Ops:
  18.3 1072.0 %while.46 = (s32[]{:T(128)}, bf16[2,2,512,768]{3,2,1,0:T(8,128)(2,1)}, bf16[2,2,32,768]{3,2,1,0:T(8,128)(2,1)S(1)}, bf16[2,2,512,6,64]{2,1,4,3,0:T(2,128)(2,1)},...) while((s32[]{:T(128)}, ...), condition=%wide.region_10.11_spmd.clone, body=%wide.region_0.10_spmd.clone.sunk | while | flops 8542994944 | bytes 398459968 | solution.py:179
  43.5 228.5 %all-reduce.21.cloned.1.call-done = bf16[3541248]{0:T(1024)(128)(2,1)} async-done(((bf16[3541248]{0:T(1024)(128)(2,1)}), bf16[3541248]{0:T(1024)(128)(2,1)}) %all-reduce.21.cloned.1.call-update) | async-done | bytes 7082512 | tf_op jit(solution)/shard_map/while
  272.0 69.0 %reshape.574 = bf16[1,3541248]{1,0:T(2,128)(2,1)S(1)} reshape(bf16[3541248]{0:T(1024)(128)(2,1)} %all-reduce.21.cloned.1.call-done) | data formatting | bytes 14164992 | tf_op jit(solution)/shard_map/while
  351.7 35.6 %slice_reduce_fusion.27 = bf16[884736]{0:T(1024)(128)(2,1)} fusion(bf16[1,3541248]{1,0:T(2,128)(2,1)S(1)} %reshape.574), kind=kLoop, calls=%fused_computation.30.clone.1 | loop fusion | bytes 3538944 | tf_op jit(solution)/shard_map/while/body/eval_jaxpr/slice | solution.py:43
  429.7 53.2 %slice_reduce_fusion.26 = (bf16[1179648]{0:T(1024)(128)(2,1)}, bf16[1179648]{0:T(1024)(128)(2,1)}) fusion(bf16[1,3541248]{1,0:T(2,128)(2,1)} %copy-done.2), kind=kLoop, calls=%fused_computation.28.clone.1 | loop fusion | bytes 9437184 | tf_op jit(solution)/shard_map/while/body/eval_jaxpr/slice | solution.py:43
  503.0 17.9 bitcast_dynamic-update-slice_fusion.12
  579.2 227.0 %all-reduce.21.cloned.1.call-done = bf16[3541248]{0:T(1024)(128)(2,1)} async-done(((bf16[3541248]{0:T(1024)(128)(2,1)}), bf16[3541248]{0:T(1024)(128)(2,1)}) %all-reduce.21.cloned.1.call-update) | async-done | bytes 7082512 | tf_op jit(solution)/shard_map/while
  806.2 68.9 %reshape.574 = bf16[1,3541248]{1,0:T(2,128)(2,1)S(1)} reshape(bf16[3541248]{0:T(1024)(128)(2,1)} %all-reduce.21.cloned.1.call-done) | data formatting | bytes 14164992 | tf_op jit(solution)/shard_map/while
  885.8 35.6 %slice_reduce_fusion.27 = bf16[884736]{0:T(1024)(128)(2,1)} fusion(bf16[1,3541248]{1,0:T(2,128)(2,1)S(1)} %reshape.574), kind=kLoop, calls=%fused_computation.30.clone.1 | loop fusion | bytes 3538944 | tf_op jit(solution)/shard_map/while/body/eval_jaxpr/slice | solution.py:43
  963.8 53.2 %slice_reduce_fusion.26 = (bf16[1179648]{0:T(1024)(128)(2,1)}, bf16[1179648]{0:T(1024)(128)(2,1)}) fusion(bf16[1,3541248]{1,0:T(2,128)(2,1)} %copy-done.2), kind=kLoop, calls=%fused_computation.28.clone.1 | loop fusion | bytes 9437184 | tf_op jit(solution)/shard_map/while/body/eval_jaxpr/slice | solution.py:43
  1037.1 17.9 bitcast_dynamic-update-slice_fusion.12
  1124.7 2047.9 %while.47 = (s32[]{:T(128)}, f32[6,768]{1,0:T(8,128)}, f32[1,221328]{1,0:T(1,128)}, f32[2,1024,768]{2,1,0:T(8,128)}, f32[2,1024,768]{2,1,0:T(8,128)}, /*index=5*...) while((s32[]{:T(128)}, f32[6,768]{1,0:T(8,128)}, ...), condition=%wide.region_36.37_spmd.clone, body=%wide.region_14.36_spmd.clone.sunk | while | flops 17043947520 | bytes 761370240 | solution.py:311
  1192.5 181.0 %all-reduce.27.cloned.1.call-done = bf16[3541248]{0:T(1024)(128)(2,1)} async-done(((bf16[3541248]{0:T(1024)(128)(2,1)}), bf16[3541248]{0:T(1024)(128)(2,1)}) %all-reduce.27.cloned.1.call-update) | async-done | bytes 7082512 | tf_op jit(solution)/shard_map/while
  1373.5 68.6 %reshape.582 = bf16[1,3541248]{1,0:T(2,128)(2,1)} reshape(bf16[3541248]{0:T(1024)(128)(2,1)} %all-reduce.27.cloned.1.call-done) | data formatting | bytes 14164992 | tf_op jit(solution)/shard_map/while
  1442.1 53.6 %slice_reduce_fusion.30 = (bf16[1179648]{0:T(1024)(128)(2,1)}, bf16[1179648]{0:T(1024)(128)(2,1)}) fusion(bf16[1,3541248]{1,0:T(2,128)(2,1)} %reshape.582), kind=kLoop, calls=%fused_computation.138.clone.1 | loop fusion | bytes 9437184 | tf_op jit(solution)/shard_map/while/body/eval_jaxpr/slice | solution.py:43
  1506.5 19.6 convert_reduce_fusion.15
  1531.6 11.8 slice_reduce_fusion.31
  1545.7 36.6 %slice_reduce_fusion.32 = bf16[884736]{0:T(1024)(128)(2,1)} fusion(bf16[1,3541248]{1,0:T(2,128)(2,1)} %reshape.582), kind=kLoop, calls=%fused_computation.141.clone.1 | loop fusion | bytes 3538944 | tf_op jit(solution)/shard_map/while/body/eval_jaxpr/slice | solution.py:43
  1626.1 11.4 multiply_reduce_fusion.27
  1691.6 54.1 %broadcast_in_dim.266 = f32[1,3541248]{1,0:T(1,128)} reshape(f32[3541248]{0:T(1024)} %constant_dynamic-update-slice_fusion.42) | data formatting | bytes 28329984 | tf_op jit(solution)/shard_map/while/body/eval_jaxpr/broadcast_in_dim | solution.py:286
  1750.8 391.5 %all-reduce.31.cloned.1.call-done = f32[1,3541248]{1,0:T(1,128)} async-done(((f32[1,3541248]{1,0:T(1,128)}), f32[1,3541248]{1,0:T(1,128)}) %all-reduce.31.cloned.1.call-update) | async-done | bytes 14165008 | tf_op jit(solution)/shard_map/while
  2213.9 182.4 %all-reduce.27.cloned.1.call-done = bf16[3541248]{0:T(1024)(128)(2,1)} async-done(((bf16[3541248]{0:T(1024)(128)(2,1)}), bf16[3541248]{0:T(1024)(128)(2,1)}) %all-reduce.27.cloned.1.call-update) | async-done | bytes 7082512 | tf_op jit(solution)/shard_map/while
  2396.3 68.6 %reshape.582 = bf16[1,3541248]{1,0:T(2,128)(2,1)} reshape(bf16[3541248]{0:T(1024)(128)(2,1)} %all-reduce.27.cloned.1.call-done) | data formatting | bytes 14164992 | tf_op jit(solution)/shard_map/while
  2464.9 53.3 %slice_reduce_fusion.30 = (bf16[1179648]{0:T(1024)(128)(2,1)}, bf16[1179648]{0:T(1024)(128)(2,1)}) fusion(bf16[1,3541248]{1,0:T(2,128)(2,1)} %reshape.582), kind=kLoop, calls=%fused_computation.138.clone.1 | loop fusion | bytes 9437184 | tf_op jit(solution)/shard_map/while/body/eval_jaxpr/slice | solution.py:43
  2529.1 19.6 convert_reduce_fusion.15
  2554.2 11.9 slice_reduce_fusion.31
  2568.4 36.6 %slice_reduce_fusion.32 = bf16[884736]{0:T(1024)(128)(2,1)} fusion(bf16[1,3541248]{1,0:T(2,128)(2,1)} %reshape.582), kind=kLoop, calls=%fused_computation.141.clone.1 | loop fusion | bytes 3538944 | tf_op jit(solution)/shard_map/while/body/eval_jaxpr/slice | solution.py:43
  2648.9 11.4 multiply_reduce_fusion.27
  2714.4 54.1 %broadcast_in_dim.266 = f32[1,3541248]{1,0:T(1,128)} reshape(f32[3541248]{0:T(1024)} %constant_dynamic-update-slice_fusion.42) | data formatting | bytes 28329984 | tf_op jit(solution)/shard_map/while/body/eval_jaxpr/broadcast_in_dim | solution.py:286
  2773.6 391.5 %all-reduce.31.cloned.1.call-done = f32[1,3541248]{1,0:T(1,128)} async-done(((f32[1,3541248]{1,0:T(1,128)}), f32[1,3541248]{1,0:T(1,128)}) %all-reduce.31.cloned.1.call-update) | async-done | bytes 14165008 | tf_op jit(solution)/shard_map/while
  3176.1 39.5 %psum.42 = f32[]{:T(128)} all-reduce(f32[]{:T(128)} %multiply_reduce_fusion.9), channel_id=1, replica_groups=mesh['dp'=16,'mp'=2] {'dp','mp'}, use_global_device_ids=true, to_apply=%region_38.39 | all-reduce | flops 1 | bytes 8 | tf_op jit(solution)/shard_map/psum | solution.py:320
  3215.6 75.8 %psum.43 = f32[6,768]{1,0:T(8,128)S(1)} all-reduce(f32[6,768]{1,0:T(8,128)} %get-tuple-element.221), channel_id=1, replica_groups=mesh['dp'=16,'mp'=2] {'dp'}, use_global_device_ids=true, to_apply=%region_39.40 | all-reduce | flops 4608 | bytes 36864 | tf_op jit(solution)/shard_map/psum | solution.py:319
  (565 shorter events, 701.5 us)
Async XLA Ops:
  18.3 1072.0 %copy-start.45 = (s32[128]{0:T(128)S(1)}, s32[128]{0:T(128)}, u32[]{:S(2)}) copy-start(s32[128]{0:T(128)} %add_bitcast_fusion.1) | copy-start | bytes 1540
  18.3 1079.7 %copy-start.50 = (s32[128,2]{0,1:T(2,128)S(1)}, s32[128,2]{0,1:T(2,128)}, u32[]{:S(2)}) copy-start(s32[128,2]{0,1:T(2,128)} %param.18) | copy-start | bytes 3076
  18.3 1089.5 %copy-start.46 = (s32[64]{0:T(128)S(1)}, s32[64]{0:T(128)}, u32[]{:S(2)}) copy-start(s32[64]{0:T(128)} %param.19) | copy-start | bytes 772
  18.5 253.5 %all-reduce.21.cloned.1.call-start = ((), (), s32[]{:S(2)}) async-start(), calls=%async_computation.2 | async-start | bytes 14168064 | tf_op jit(solution)/shard_map/while
  39.9 460.0 %all-reduce.23.cloned.1.call-start = ((), (), s32[]{:S(2)}) async-start(), calls=%async_computation.3 | async-start | bytes 3145728 | tf_op jit(solution)/shard_map/while/body/eval_jaxpr/psum | solution.py:149
  429.6 114.6 %all-reduce.25.cloned.1.call-start = ((), (), s32[]{:S(2)}) async-start(), calls=%async_computation.4 | async-start | bytes 3145728 | tf_op jit(solution)/shard_map/while/body/eval_jaxpr/psum | solution.py:157
  503.0 17.9 copy-start.23
  554.2 252.0 %all-reduce.21.cloned.1.call-start = ((), (), s32[]{:S(2)}) async-start(), calls=%async_computation.2 | async-start | bytes 14168064 | tf_op jit(solution)/shard_map/while
  575.6 458.4 %all-reduce.23.cloned.1.call-start = ((), (), s32[]{:S(2)}) async-start(), calls=%async_computation.3 | async-start | bytes 3145728 | tf_op jit(solution)/shard_map/while/body/eval_jaxpr/psum | solution.py:149
  963.7 114.6 %all-reduce.25.cloned.1.call-start = ((), (), s32[]{:S(2)}) async-start(), calls=%async_computation.4 | async-start | bytes 3145728 | tf_op jit(solution)/shard_map/while/body/eval_jaxpr/psum | solution.py:157
  1091.2 15.9 all-to-all-start
  1109.0 11.6 all-to-all-start.1
  1124.7 2168.8 %copy-start.43 = (f32[6,768]{1,0:T(8,128)S(1)}, f32[6,768]{1,0:T(8,128)}, u32[]{:S(2)}) copy-start(f32[6,768]{1,0:T(8,128)} %param.24) | copy-start | bytes 55300
  1124.7 2168.8 %copy-start.44 = (f32[6,768]{1,0:T(8,128)S(1)}, f32[6,768]{1,0:T(8,128)}, u32[]{:S(2)}) copy-start(f32[6,768]{1,0:T(8,128)} %param.25) | copy-start | bytes 55300
  1124.8 24.5 copy-start.34
  1124.9 51.6 %copy-start.39 = (f32[2,2,6,512,1]{3,2,1,4,0:T(8,128)}, f32[2,2,6,512,1]{3,2,1,4,0:T(8,128)S(1)}, u32[]{:S(2)}) copy-start(f32[2,2,6,512,1]{3,2,1,4,0:T(8,128)S(1)} %get-tuple-element.975) | copy-start | bytes 147460 | tf_op jit(solution)/shard_map/while
  1124.9 248.6 %all-reduce.27.cloned.1.call-start = ((), (), s32[]{:S(2)}) async-start(), calls=%async_computation.5 | async-start | bytes 14168064 | tf_op jit(solution)/shard_map/while
  1146.2 454.4 %all-reduce.29.cloned.1.call-start = ((), (), s32[]{:S(2)}) async-start(), calls=%async_computation.6 | async-start | bytes 3145728 | tf_op jit(solution)/shard_map/while/body/eval_jaxpr/psum | solution.py:242
  1506.5 21.2 copy-start.24
  1531.5 215.7 %all-reduce.33.cloned.1.call-start = ((), (), s32[]{:S(2)}) async-start(), calls=%async_computation.8 | async-start | bytes 3145728 | tf_op jit(solution)/shard_map/while/body/eval_jaxpr/psum | solution.py:282
  1663.0 479.2 %all-reduce.31.cloned.1.call-start = ((), (), s32[]{:S(2)}) async-start(), calls=%async_computation.7 | async-start | bytes 28329984 | tf_op jit(solution)/shard_map/while
  1747.2 398.8 %copy-start.35 = (f32[6,768]{1,0:T(8,128)S(1)}, f32[6,768]{1,0:T(8,128)}, u32[]{:S(2)}) copy-start(f32[6,768]{1,0:T(8,128)} %copy-done.34) | copy-start | bytes 55300 | tf_op jit(solution)/shard_map/while
  1747.3 398.8 %copy-start.40 = (f32[2,2,6,512,1]{3,2,1,4,0:T(8,128)S(1)}, f32[2,2,6,512,1]{3,2,1,4,0:T(8,128)}, u32[]{:S(2)}) copy-start(f32[2,2,6,512,1]{3,2,1,4,0:T(8,128)} %copy-done.39) | copy-start | bytes 147460 | tf_op jit(solution)/shard_map/while
  2146.3 24.5 copy-start.34
  2146.3 51.8 %copy-start.39 = (f32[2,2,6,512,1]{3,2,1,4,0:T(8,128)}, f32[2,2,6,512,1]{3,2,1,4,0:T(8,128)S(1)}, u32[]{:S(2)}) copy-start(f32[2,2,6,512,1]{3,2,1,4,0:T(8,128)S(1)} %get-tuple-element.975) | copy-start | bytes 147460 | tf_op jit(solution)/shard_map/while
  2146.3 250.0 %all-reduce.27.cloned.1.call-start = ((), (), s32[]{:S(2)}) async-start(), calls=%async_computation.5 | async-start | bytes 14168064 | tf_op jit(solution)/shard_map/while
  2167.7 455.8 %all-reduce.29.cloned.1.call-start = ((), (), s32[]{:S(2)}) async-start(), calls=%async_computation.6 | async-start | bytes 3145728 | tf_op jit(solution)/shard_map/while/body/eval_jaxpr/psum | solution.py:242
  2529.1 21.2 copy-start.24
  2554.1 215.9 %all-reduce.33.cloned.1.call-start = ((), (), s32[]{:S(2)}) async-start(), calls=%async_computation.8 | async-start | bytes 3145728 | tf_op jit(solution)/shard_map/while/body/eval_jaxpr/psum | solution.py:282
  2685.8 479.3 %all-reduce.31.cloned.1.call-start = ((), (), s32[]{:S(2)}) async-start(), calls=%async_computation.7 | async-start | bytes 28329984 | tf_op jit(solution)/shard_map/while
  2770.1 399.0 %copy-start.35 = (f32[6,768]{1,0:T(8,128)S(1)}, f32[6,768]{1,0:T(8,128)}, u32[]{:S(2)}) copy-start(f32[6,768]{1,0:T(8,128)} %copy-done.34) | copy-start | bytes 55300 | tf_op jit(solution)/shard_map/while
  2770.1 398.9 %copy-start.40 = (f32[2,2,6,512,1]{3,2,1,4,0:T(8,128)S(1)}, f32[2,2,6,512,1]{3,2,1,4,0:T(8,128)}, u32[]{:S(2)}) copy-start(f32[2,2,6,512,1]{3,2,1,4,0:T(8,128)} %copy-done.39) | copy-start | bytes 147460 | tf_op jit(solution)/shard_map/while
  (90 other events, 392.3 us)
Sparse Core Ops, SparseCore 0:
  40.0 231.9 all-reduce.20
  429.8 19.4 all-reduce.22
  524.8 19.4 all-reduce.24
  575.7 230.4 all-reduce.20
  963.9 19.4 all-reduce.22
  1058.8 19.4 all-reduce.24
  1146.4 227.0 all-reduce.26
  1531.7 19.4 all-reduce.28
  1663.2 19.4 all-reduce.32
  1745.9 396.3 all-reduce.30
  2167.8 228.4 all-reduce.26
  2554.3 19.4 all-reduce.28
  2686.0 19.4 all-reduce.32
  2768.7 396.4 all-reduce.30
where the time goes:
time: 3320 us; the launch traced here: 3310 us
  waiting for transfers between devices  1640 us (49%)
  local copies, waits for them, and re-layouts  1090 us (33%)
  matrix products  253 us (8%)
  other arithmetic  169 us (5%)
  blocking collectives  115 us (3%)
    while x20, waiting for transfers between devices  1600 us
    slice x12, local copies, waits for them, and re-layouts, unpack(): packed[offset:offset + height * extent].reshape(height, extent)  403 us
    while x242, local copies, waits for them, and re-layouts  374 us
    broadcast_in_dim x2, local copies, waits for them, and re-layouts, backward_step(): jnp.concatenate([w_qkv_grad.reshape(-1), w_attn_grad.reshape(-1), w_in_gr...  108 us
    psum x1, blocking collectives, per_device(): shared_total = lax.psum(shared_acc, 'dp')  75.8 us
    reshape x16, local copies, waits for them, and re-layouts, unpack(): packed[offset:offset + height * extent].reshape(height, extent)  70.3 us
  transfers between devices with their start and end apart: 16, of which 10 were waited for; matrix products, arithmetic and copies ran while one was open for 17% of the time, Pallas kernels for 0%

commit v1 on v0

--- a/solution.py
+++ b/solution.py
@@ -316,7 +316,12 @@
     flat_grad = flat_acc
     flat_grad = flat_grad / LOSS_SCALE
     local_squares = jnp.sum(flat_grad * flat_grad)
-    shared_total = lax.psum(shared_acc, "dp")
+    ndev = lax.axis_size("dp")
+    shared_total, shaped = (shared_acc, 0)
+    while 1 << shaped < ndev:
+        val = lax.ppermute(shared_total, "dp", [(i, i ^ 1 << shaped) for i in range(ndev)])
+        shared_total = shared_total + val
+        shaped = shaped + 1
     total_squares = lax.psum(local_squares, ("dp", "mp"))
     shared_grad = shared_total / LOSS_SCALE
     norm_value = jnp.sqrt(total_squares + jnp.sum(shared_grad * shared_grad))

time: 3320 us -> 3260 us (0.982)
  blocking collectives: 115 us -> 39.6 us
    psum x1 -> x0, blocking collectives: 75.8 us -> none  [per_device(): shared_total = lax.psum(shared_acc, 'dp')]
  transfers between devices with their start and end apart: 16 -> 20, of which waited for: 10 -> 13; matrix products, arithmetic and copies ran while one was open for 17% -> 17% of each run, Pallas kernels for 0% -> 0%
where the time goes in v1:
time: 3260 us; the launch traced here: 3250 us
  waiting for transfers between devices  1650 us (51%)
  local copies, waits for them, and re-layouts  1090 us (33%)
  matrix products  253 us (8%)
  other arithmetic  170 us (5%)
  blocking collectives  39.6 us (1%)
    while x20, waiting for transfers between devices  1600 us
    slice x12, local copies, waits for them, and re-layouts, unpack(): packed[offset:offset + height * extent].reshape(height, extent)  403 us
    while x242, local copies, waits for them, and re-layouts  374 us
    broadcast_in_dim x2, local copies, waits for them, and re-layouts, backward_step(): jnp.concatenate([w_qkv_grad.reshape(-1), w_attn_grad.reshape(-1), w_in_gr...  108 us
    reshape x16, local copies, waits for them, and re-layouts, unpack(): packed[offset:offset + height * extent].reshape(height, extent)  70.3 us
  transfers between devices with their start and end apart: 20, of which 13 were waited for; matrix products, arithmetic and copies ran while one was open for 17% of the time, Pallas kernels for 0%

profile of v1, /device:TPU:0, one launch (start us, length us, event | category | flops | bytes accessed | tf_op | source)
XLA Modules:
  0.0 3249.2 jit_solution(8424791393531339129)
XLA Ops:
  18.3 1072.0 %while.46 = (s32[]{:T(128)}, bf16[2,2,512,768]{3,2,1,0:T(8,128)(2,1)}, bf16[2,2,32,768]{3,2,1,0:T(8,128)(2,1)S(1)}, bf16[2,2,512,6,64]{2,1,4,3,0:T(2,128)(2,1)},...) while((s32[]{:T(128)}, ...), condition=%wide.region_10.11_spmd.clone, body=%wide.region_0.10_spmd.clone.sunk | while | flops 8542994944 | bytes 398459968 | solution.py:179
  43.5 228.5 %all-reduce.21.cloned.1.call-done = bf16[3541248]{0:T(1024)(128)(2,1)} async-done(((bf16[3541248]{0:T(1024)(128)(2,1)}), bf16[3541248]{0:T(1024)(128)(2,1)}) %all-reduce.21.cloned.1.call-update) | async-done | bytes 7082512 | tf_op jit(solution)/shard_map/while
  272.0 69.0 %reshape.574 = bf16[1,3541248]{1,0:T(2,128)(2,1)S(1)} reshape(bf16[3541248]{0:T(1024)(128)(2,1)} %all-reduce.21.cloned.1.call-done) | data formatting | bytes 14164992 | tf_op jit(solution)/shard_map/while
  351.7 35.6 %slice_reduce_fusion.27 = bf16[884736]{0:T(1024)(128)(2,1)} fusion(bf16[1,3541248]{1,0:T(2,128)(2,1)S(1)} %reshape.574), kind=kLoop, calls=%fused_computation.30.clone.1 | loop fusion | bytes 3538944 | tf_op jit(solution)/shard_map/while/body/eval_jaxpr/slice | solution.py:43
  429.7 53.2 %slice_reduce_fusion.26 = (bf16[1179648]{0:T(1024)(128)(2,1)}, bf16[1179648]{0:T(1024)(128)(2,1)}) fusion(bf16[1,3541248]{1,0:T(2,128)(2,1)} %copy-done.2), kind=kLoop, calls=%fused_computation.28.clone.1 | loop fusion | bytes 9437184 | tf_op jit(solution)/shard_map/while/body/eval_jaxpr/slice | solution.py:43
  503.0 17.9 bitcast_dynamic-update-slice_fusion.12
  579.2 227.0 %all-reduce.21.cloned.1.call-done = bf16[3541248]{0:T(1024)(128)(2,1)} async-done(((bf16[3541248]{0:T(1024)(128)(2,1)}), bf16[3541248]{0:T(1024)(128)(2,1)}) %all-reduce.21.cloned.1.call-update) | async-done | bytes 7082512 | tf_op jit(solution)/shard_map/while
  806.2 68.9 %reshape.574 = bf16[1,3541248]{1,0:T(2,128)(2,1)S(1)} reshape(bf16[3541248]{0:T(1024)(128)(2,1)} %all-reduce.21.cloned.1.call-done) | data formatting | bytes 14164992 | tf_op jit(solution)/shard_map/while
  885.8 35.6 %slice_reduce_fusion.27 = bf16[884736]{0:T(1024)(128)(2,1)} fusion(bf16[1,3541248]{1,0:T(2,128)(2,1)S(1)} %reshape.574), kind=kLoop, calls=%fused_computation.30.clone.1 | loop fusion | bytes 3538944 | tf_op jit(solution)/shard_map/while/body/eval_jaxpr/slice | solution.py:43
  963.8 53.2 %slice_reduce_fusion.26 = (bf16[1179648]{0:T(1024)(128)(2,1)}, bf16[1179648]{0:T(1024)(128)(2,1)}) fusion(bf16[1,3541248]{1,0:T(2,128)(2,1)} %copy-done.2), kind=kLoop, calls=%fused_computation.28.clone.1 | loop fusion | bytes 9437184 | tf_op jit(solution)/shard_map/while/body/eval_jaxpr/slice | solution.py:43
  1037.1 17.9 bitcast_dynamic-update-slice_fusion.12
  1067.0 11.3 all-reduce.25.cloned.1.call-done
  1124.7 2047.9 %while.47 = (s32[]{:T(128)}, f32[6,768]{1,0:T(8,128)}, f32[1,221328]{1,0:T(1,128)}, f32[2,1024,768]{2,1,0:T(8,128)}, f32[2,1024,768]{2,1,0:T(8,128)}, /*index=5*...) while((s32[]{:T(128)}, f32[6,768]{1,0:T(8,128)}, ...), condition=%wide.region_36.37_spmd.clone, body=%wide.region_14.36_spmd.clone.sunk | while | flops 17043947520 | bytes 761370240 | solution.py:311
  1192.4 181.1 %all-reduce.27.cloned.1.call-done = bf16[3541248]{0:T(1024)(128)(2,1)} async-done(((bf16[3541248]{0:T(1024)(128)(2,1)}), bf16[3541248]{0:T(1024)(128)(2,1)}) %all-reduce.27.cloned.1.call-update) | async-done | bytes 7082512 | tf_op jit(solution)/shard_map/while
  1373.5 68.6 %reshape.582 = bf16[1,3541248]{1,0:T(2,128)(2,1)} reshape(bf16[3541248]{0:T(1024)(128)(2,1)} %all-reduce.27.cloned.1.call-done) | data formatting | bytes 14164992 | tf_op jit(solution)/shard_map/while
  1442.1 53.6 %slice_reduce_fusion.30 = (bf16[1179648]{0:T(1024)(128)(2,1)}, bf16[1179648]{0:T(1024)(128)(2,1)}) fusion(bf16[1,3541248]{1,0:T(2,128)(2,1)} %reshape.582), kind=kLoop, calls=%fused_computation.138.clone.1 | loop fusion | bytes 9437184 | tf_op jit(solution)/shard_map/while/body/eval_jaxpr/slice | solution.py:43
  1506.5 19.5 convert_reduce_fusion.15
  1531.6 11.8 slice_reduce_fusion.31
  1545.7 36.6 %slice_reduce_fusion.32 = bf16[884736]{0:T(1024)(128)(2,1)} fusion(bf16[1,3541248]{1,0:T(2,128)(2,1)} %reshape.582), kind=kLoop, calls=%fused_computation.141.clone.1 | loop fusion | bytes 3538944 | tf_op jit(solution)/shard_map/while/body/eval_jaxpr/slice | solution.py:43
  1626.0 11.4 multiply_reduce_fusion.27
  1691.5 54.1 %broadcast_in_dim.266 = f32[1,3541248]{1,0:T(1,128)} reshape(f32[3541248]{0:T(1024)} %constant_dynamic-update-slice_fusion.42) | data formatting | bytes 28329984 | tf_op jit(solution)/shard_map/while/body/eval_jaxpr/broadcast_in_dim | solution.py:286
  1750.8 391.5 %all-reduce.31.cloned.1.call-done = f32[1,3541248]{1,0:T(1,128)} async-done(((f32[1,3541248]{1,0:T(1,128)}), f32[1,3541248]{1,0:T(1,128)}) %all-reduce.31.cloned.1.call-update) | async-done | bytes 14165008 | tf_op jit(solution)/shard_map/while
  2213.9 182.4 %all-reduce.27.cloned.1.call-done = bf16[3541248]{0:T(1024)(128)(2,1)} async-done(((bf16[3541248]{0:T(1024)(128)(2,1)}), bf16[3541248]{0:T(1024)(128)(2,1)}) %all-reduce.27.cloned.1.call-update) | async-done | bytes 7082512 | tf_op jit(solution)/shard_map/while
  2396.3 68.6 %reshape.582 = bf16[1,3541248]{1,0:T(2,128)(2,1)} reshape(bf16[3541248]{0:T(1024)(128)(2,1)} %all-reduce.27.cloned.1.call-done) | data formatting | bytes 14164992 | tf_op jit(solution)/shard_map/while
  2464.9 53.3 %slice_reduce_fusion.30 = (bf16[1179648]{0:T(1024)(128)(2,1)}, bf16[1179648]{0:T(1024)(128)(2,1)}) fusion(bf16[1,3541248]{1,0:T(2,128)(2,1)} %reshape.582), kind=kLoop, calls=%fused_computation.138.clone.1 | loop fusion | bytes 9437184 | tf_op jit(solution)/shard_map/while/body/eval_jaxpr/slice | solution.py:43
  2529.1 19.6 convert_reduce_fusion.15
  2554.1 11.9 slice_reduce_fusion.31
  2568.3 36.6 %slice_reduce_fusion.32 = bf16[884736]{0:T(1024)(128)(2,1)} fusion(bf16[1,3541248]{1,0:T(2,128)(2,1)} %reshape.582), kind=kLoop, calls=%fused_computation.141.clone.1 | loop fusion | bytes 3538944 | tf_op jit(solution)/shard_map/while/body/eval_jaxpr/slice | solution.py:43
  2648.8 11.4 multiply_reduce_fusion.27
  2714.4 54.1 %broadcast_in_dim.266 = f32[1,3541248]{1,0:T(1,128)} reshape(f32[3541248]{0:T(1024)} %constant_dynamic-update-slice_fusion.42) | data formatting | bytes 28329984 | tf_op jit(solution)/shard_map/while/body/eval_jaxpr/broadcast_in_dim | solution.py:286
  2773.6 391.5 %all-reduce.31.cloned.1.call-done = f32[1,3541248]{1,0:T(1,128)} async-done(((f32[1,3541248]{1,0:T(1,128)}), f32[1,3541248]{1,0:T(1,128)}) %all-reduce.31.cloned.1.call-update) | async-done | bytes 14165008 | tf_op jit(solution)/shard_map/while
  3190.1 39.6 %psum.35 = f32[]{:T(128)} all-reduce(f32[]{:T(128)} %multiply_reduce_fusion.9), channel_id=1, replica_groups=mesh['dp'=16,'mp'=2] {'dp','mp'}, use_global_device_ids=true, to_apply=%region_38.39 | all-reduce | flops 1 | bytes 8 | tf_op jit(solution)/shard_map/psum | solution.py:325
  (575 shorter events, 704.3 us)
Async XLA Ops:
  18.3 1072.0 %copy-start.45 = (s32[128]{0:T(128)S(1)}, s32[128]{0:T(128)}, u32[]{:S(2)}) copy-start(s32[128]{0:T(128)} %add_bitcast_fusion.1) | copy-start | bytes 1540
  18.3 1079.7 %copy-start.50 = (s32[128,2]{0,1:T(2,128)S(1)}, s32[128,2]{0,1:T(2,128)}, u32[]{:S(2)}) copy-start(s32[128,2]{0,1:T(2,128)} %param.18) | copy-start | bytes 3076
  18.3 1089.5 %copy-start.46 = (s32[64]{0:T(128)S(1)}, s32[64]{0:T(128)}, u32[]{:S(2)}) copy-start(s32[64]{0:T(128)} %param.19) | copy-start | bytes 772
  18.5 253.5 %all-reduce.21.cloned.1.call-start = ((), (), s32[]{:S(2)}) async-start(), calls=%async_computation.2 | async-start | bytes 14168064 | tf_op jit(solution)/shard_map/while
  39.9 460.0 %all-reduce.23.cloned.1.call-start = ((), (), s32[]{:S(2)}) async-start(), calls=%async_computation.3 | async-start | bytes 3145728 | tf_op jit(solution)/shard_map/while/body/eval_jaxpr/psum | solution.py:149
  429.6 114.6 %all-reduce.25.cloned.1.call-start = ((), (), s32[]{:S(2)}) async-start(), calls=%async_computation.4 | async-start | bytes 3145728 | tf_op jit(solution)/shard_map/while/body/eval_jaxpr/psum | solution.py:157
  554.2 252.0 %all-reduce.21.cloned.1.call-start = ((), (), s32[]{:S(2)}) async-start(), calls=%async_computation.2 | async-start | bytes 14168064 | tf_op jit(solution)/shard_map/while
  575.6 458.4 %all-reduce.23.cloned.1.call-start = ((), (), s32[]{:S(2)}) async-start(), calls=%async_computation.3 | async-start | bytes 3145728 | tf_op jit(solution)/shard_map/while/body/eval_jaxpr/psum | solution.py:149
  963.7 114.6 %all-reduce.25.cloned.1.call-start = ((), (), s32[]{:S(2)}) async-start(), calls=%async_computation.4 | async-start | bytes 3145728 | tf_op jit(solution)/shard_map/while/body/eval_jaxpr/psum | solution.py:157
  1091.2 15.9 all-to-all-start
  1109.0 11.6 all-to-all-start.1
  1124.8 24.5 copy-start.34
  1124.8 51.6 %copy-start.39 = (f32[2,2,6,512,1]{3,2,1,4,0:T(8,128)}, f32[2,2,6,512,1]{3,2,1,4,0:T(8,128)S(1)}, u32[]{:S(2)}) copy-start(f32[2,2,6,512,1]{3,2,1,4,0:T(8,128)S(1)} %get-tuple-element.977) | copy-start | bytes 147460 | tf_op jit(solution)/shard_map/while
  1124.9 248.6 %all-reduce.27.cloned.1.call-start = ((), (), s32[]{:S(2)}) async-start(), calls=%async_computation.5 | async-start | bytes 14168064 | tf_op jit(solution)/shard_map/while
  1146.2 454.3 %all-reduce.29.cloned.1.call-start = ((), (), s32[]{:S(2)}) async-start(), calls=%async_computation.6 | async-start | bytes 3145728 | tf_op jit(solution)/shard_map/while/body/eval_jaxpr/psum | solution.py:242
  1531.5 215.7 %all-reduce.33.cloned.1.call-start = ((), (), s32[]{:S(2)}) async-start(), calls=%async_computation.8 | async-start | bytes 3145728 | tf_op jit(solution)/shard_map/while/body/eval_jaxpr/psum | solution.py:282
  1663.0 479.2 %all-reduce.31.cloned.1.call-start = ((), (), s32[]{:S(2)}) async-start(), calls=%async_computation.7 | async-start | bytes 28329984 | tf_op jit(solution)/shard_map/while
  1747.2 398.8 %copy-start.35 = (f32[6,768]{1,0:T(8,128)S(1)}, f32[6,768]{1,0:T(8,128)}, u32[]{:S(2)}) copy-start(f32[6,768]{1,0:T(8,128)} %copy-done.34) | copy-start | bytes 55300 | tf_op jit(solution)/shard_map/while
  1747.2 398.8 %copy-start.40 = (f32[2,2,6,512,1]{3,2,1,4,0:T(8,128)S(1)}, f32[2,2,6,512,1]{3,2,1,4,0:T(8,128)}, u32[]{:S(2)}) copy-start(f32[2,2,6,512,1]{3,2,1,4,0:T(8,128)} %copy-done.39) | copy-start | bytes 147460 | tf_op jit(solution)/shard_map/while
  2146.2 24.5 copy-start.34
  2146.2 51.8 %copy-start.39 = (f32[2,2,6,512,1]{3,2,1,4,0:T(8,128)}, f32[2,2,6,512,1]{3,2,1,4,0:T(8,128)S(1)}, u32[]{:S(2)}) copy-start(f32[2,2,6,512,1]{3,2,1,4,0:T(8,128)S(1)} %get-tuple-element.977) | copy-start | bytes 147460 | tf_op jit(solution)/shard_map/while
  2146.2 250.0 %all-reduce.27.cloned.1.call-start = ((), (), s32[]{:S(2)}) async-start(), calls=%async_computation.5 | async-start | bytes 14168064 | tf_op jit(solution)/shard_map/while
  2167.6 455.8 %all-reduce.29.cloned.1.call-start = ((), (), s32[]{:S(2)}) async-start(), calls=%async_computation.6 | async-start | bytes 3145728 | tf_op jit(solution)/shard_map/while/body/eval_jaxpr/psum | solution.py:242
  2529.1 21.2 copy-start.24
  2554.1 215.9 %all-reduce.33.cloned.1.call-start = ((), (), s32[]{:S(2)}) async-start(), calls=%async_computation.8 | async-start | bytes 3145728 | tf_op jit(solution)/shard_map/while/body/eval_jaxpr/psum | solution.py:282
  2685.8 479.3 %all-reduce.31.cloned.1.call-start = ((), (), s32[]{:S(2)}) async-start(), calls=%async_computation.7 | async-start | bytes 28329984 | tf_op jit(solution)/shard_map/while
  2770.0 399.0 %copy-start.35 = (f32[6,768]{1,0:T(8,128)S(1)}, f32[6,768]{1,0:T(8,128)}, u32[]{:S(2)}) copy-start(f32[6,768]{1,0:T(8,128)} %copy-done.34) | copy-start | bytes 55300 | tf_op jit(solution)/shard_map/while
  2770.0 398.9 %copy-start.40 = (f32[2,2,6,512,1]{3,2,1,4,0:T(8,128)S(1)}, f32[2,2,6,512,1]{3,2,1,4,0:T(8,128)}, u32[]{:S(2)}) copy-start(f32[2,2,6,512,1]{3,2,1,4,0:T(8,128)} %copy-done.39) | copy-start | bytes 147460 | tf_op jit(solution)/shard_map/while
  3172.6 4.1 collective-permute-start
  3177.5 3.8 collective-permute-start.1
  3181.3 4.1 collective-permute-start.2
  3185.4 44.4 %collective-permute-start.3 = (f32[6,768]{1,0:T(8,128)S(1)}, f32[6,768]{1,0:T(8,128)S(1)}, u32[]{:S(2)}, u32[]{:S(2)}) collective-permute-start(f32[6,768]{1,0:T(8,128)S(1)} %add.258), channel_id=1, source_target_pairs={{0,16},{2,18},{4,20},{6,22},{8,24},{10,26},{12,28},{14,30},{16,0},... | collective-permute-start | bytes 55304 | tf_op jit(solution)/shard_map/ppermute | solution.py:322
  (94 other events, 449.1 us)
Sparse Core Ops, SparseCore 0:
  40.0 231.9 all-reduce.20
  429.8 19.4 all-reduce.22
  524.8 19.4 all-reduce.24
  575.7 230.4 all-reduce.20
  963.9 19.4 all-reduce.22
  1058.8 19.4 all-reduce.24
  1146.4 227.0 all-reduce.26
  1531.6 19.4 all-reduce.28
  1663.1 19.4 all-reduce.32
  1745.8 396.3 all-reduce.30
  2167.7 228.4 all-reduce.26
  2554.2 19.4 all-reduce.28
  2685.9 19.4 all-reduce.32
  2768.6 396.3 all-reduce.30
